TPU v7x, 32 devices: a whole 2x2x4 slice. The times are simulated.
32 devices in a mesh: dp: 8 (over z, x), neg: 4 (over y, core).
Axes of the slice: x: 2, y: 2, z: 4, core: 2. Of those that a mesh axis runs over, the one named last changes fastest.
Arguments:
- history: bfloat16 [6144, 512], P('dp'), may hold values from -6 to 6
- lengths: int32 [16], P('dp'), may hold values from 1 to 384
- w_in: bfloat16 [512, 2048], P(None, 'neg'), may hold values from -0.25 to 0.25
- w_out: bfloat16 [512, 512], P('neg'), may hold values from -0.25 to 0.25
- target_ids: int32 [6144], P('dp'), may hold values from 0 to 8191
- negative_ids: int32 [16384], P('neg'), may hold values from 0 to 8191, as said below
- item_table: bfloat16 [8192, 512], P('neg'), may hold values from -6 to 6
Outputs:
- token_loss: float32 [6144], P('dp')
- grad_w_in: float32 [512, 2048], P('dp', 'neg')
- grad_w_out: float32 [512, 512], P('neg', 'dp')
- grad_table: float32 [8192, 512], P(('neg', 'dp'))
Inputs may be any that keep to these rules, and one draw needn't show every extreme that they name: `negative_ids`: negative n names one of the rows (n // 4096) * 2048 to (n // 4096 + 1) * 2048 - 1.
All inputs are finite; a program needn't handle non-finite values.
Results may differ from a plain program's by a relative error of at most 0.0098.
Values may be sent and summed in bfloat16 or wider, within the bound.
A program may use at most 128 MiB of HBM per device.

v0:
```python
import jax
import jax.numpy as jnp
from jax import lax
from jax.sharding import PartitionSpec as P

HEAD = 64


logit_scale = 64.0
epsilon = 1e-06


def silu_grad(values):
    logistic = jax.nn.sigmoid(values)
    return logistic * (1.0 + values * (1.0 - logistic))


def moment_norm(values):
    row_mean = jnp.mean(values, -1, keepdims=True)
    row_square = jnp.mean(values * values, -1, keepdims=True)
    norm_scale = lax.rsqrt(row_square - row_mean * row_mean + epsilon)
    return ((values - row_mean) * norm_scale, norm_scale)


def normalize_rows(values):
    inverse = lax.rsqrt(jnp.sum(values * values, -1, keepdims=True) + epsilon)
    return (values * inverse, inverse)


def project_rows(raw_rows, unit_part, inverse):
    return (raw_rows - unit_part * jnp.sum(raw_rows * unit_part, -1, keepdims=True)) * inverse


def segment_rows(values, slots, first_row, row_count):
    inside = (slots >= first_row) & (slots < first_row + row_count)
    placed = jnp.where(inside, slots - first_row, row_count)
    return jax.ops.segment_sum(values, placed, row_count + 1)[:row_count]


def on_device(history, lengths, w_in, w_out, target_ids, negative_ids, item_table):
    tok_rows, model_width = history.shape
    user_count = lengths.shape[0]
    hist_len = tok_rows // user_count
    local_heads = w_in.shape[1] // (4 * HEAD)
    local_width = local_heads * HEAD
    item_rows = item_table.shape[0]
    groups = lax.axis_size("neg")
    share_rows = tok_rows // groups
    share_start = lax.axis_index("neg") * share_rows
    item_base = lax.axis_index("neg") * item_rows
    inputs_float = history.astype(jnp.float32)
    normed = moment_norm(inputs_float)[0].astype(jnp.bfloat16)
    pre_act = jnp.dot(normed, w_in, preferred_element_type=jnp.float32)
    projected = (
        jax.nn.silu(pre_act)
        .astype(jnp.bfloat16)
        .reshape(user_count, hist_len, local_heads, 4, HEAD)
    )
    gate_rows = projected[:, :, :, 0]
    value_rows = projected[:, :, :, 1]
    query_rows = projected[:, :, :, 2]
    key_rows = projected[:, :, :, 3]
    scores = jnp.einsum("bihd,bjhd->bhij", query_rows, key_rows, preferred_element_type=jnp.float32)
    position = jnp.arange(hist_len, dtype=jnp.int32)
    live_slots = position[None, :] < lengths[:, None]
    causal = position[None, :] <= position[:, None]
    attn_mask = (causal[None] & live_slots[:, :, None]).astype(jnp.float32)[:, None]
    attn_weights = (jax.nn.silu(scores) * attn_mask / hist_len).astype(jnp.bfloat16)
    attended = jnp.einsum(
        "bhij,bjhd->bihd", attn_weights, value_rows, preferred_element_type=jnp.float32
    ).reshape(tok_rows, local_width)
    head_sums = lax.psum((jnp.sum(attended, -1), jnp.sum(attended * attended, -1)), "neg")
    row_mean = head_sums[0][:, None] / model_width
    norm_scale = lax.rsqrt(head_sums[1][:, None] / model_width - row_mean * row_mean + epsilon)
    centred = (attended - row_mean) * norm_scale
    gate_flat = gate_rows.reshape(tok_rows, local_width).astype(jnp.float32)
    mixed_rows = (centred * gate_flat).astype(jnp.bfloat16)
    branch = jnp.dot(mixed_rows, w_out, preferred_element_type=jnp.float32)
    branch_part = lax.psum_scatter(branch, "neg", scatter_dimension=0, tiled=True)
    inputs_part = lax.dynamic_slice_in_dim(inputs_float, share_start, share_rows, 0)
    user_unit, user_inverse = normalize_rows(inputs_part + branch_part)
    user_rounded = lax.all_gather(user_unit.astype(jnp.bfloat16), "neg", axis=0, tiled=True)
    item_unit, item_inverse = normalize_rows(item_table.astype(jnp.float32))
    neg_local = negative_ids - item_base
    neg_rounded = item_unit.astype(jnp.bfloat16)[neg_local]
    target_local = target_ids - item_base
    owned_rows = (target_local >= 0) & (target_local < item_rows)
    target_unit = jnp.where(
        owned_rows[:, None], item_unit[jnp.clip(target_local, 0, item_rows - 1)], 0.0
    )
    user_float = user_rounded.astype(jnp.float32)
    positive_part = logit_scale * jnp.sum(user_float * target_unit, -1)
    logits = logit_scale * lax.dot_general(
        user_rounded, neg_rounded, (((1,), (1,)), ((), ())), preferred_element_type=jnp.float32
    )
    exp_terms = jnp.where(target_ids[:, None] != negative_ids[None, :], jnp.exp(logits), 0.0)
    positive, negative_sum = lax.psum((positive_part, jnp.sum(exp_terms, -1)), "neg")
    partition_sum = jnp.exp(positive) + negative_sum
    live_rows = live_slots.reshape(tok_rows).astype(jnp.float32)
    token_loss = live_rows * (jnp.log(partition_sum) - positive)
    logit_grads = (live_rows[:, None] * exp_terms / partition_sum[:, None]).astype(jnp.bfloat16)
    positive_grad = live_rows * (jnp.exp(positive) / partition_sum - 1.0)
    unit_part = (
        logit_scale * jnp.dot(logit_grads, neg_rounded, preferred_element_type=jnp.float32)
        + logit_scale * positive_grad[:, None] * target_unit
    )
    unit_grad = lax.psum_scatter(unit_part, "neg", scatter_dimension=0, tiled=True)
    output_part = project_rows(unit_grad, user_unit, user_inverse).astype(jnp.bfloat16)
    output_rounded = lax.all_gather(output_part, "neg", axis=0, tiled=True)
    grad_out_local = lax.dot_general(
        mixed_rows, output_rounded, (((0,), (0,)), ((), ())), preferred_element_type=jnp.float32
    )
    mixed_grad = lax.dot_general(
        output_rounded, w_out, (((1,), (1,)), ((), ())), preferred_element_type=jnp.float32
    )
    centred_grad = mixed_grad * gate_flat
    gate_grad = mixed_grad * centred
    back_sums = lax.psum((jnp.sum(centred_grad, -1), jnp.sum(centred_grad * centred, -1)), "neg")
    attended_grad = norm_scale * (
        centred_grad
        - back_sums[0][:, None] / model_width
        - centred * back_sums[1][:, None] / model_width
    )
    attended_grad = attended_grad.astype(jnp.bfloat16).reshape(
        user_count, hist_len, local_heads, HEAD
    )
    weight_grad = jnp.einsum(
        "bihd,bjhd->bhij", attended_grad, value_rows, preferred_element_type=jnp.float32
    )
    value_grad = jnp.einsum(
        "bhij,bihd->bjhd", attn_weights, attended_grad, preferred_element_type=jnp.float32
    )
    score_grad = (weight_grad * attn_mask / hist_len * silu_grad(scores)).astype(jnp.bfloat16)
    query_grad = jnp.einsum(
        "bhij,bjhd->bihd", score_grad, key_rows, preferred_element_type=jnp.float32
    )
    key_grad = jnp.einsum(
        "bhij,bihd->bjhd", score_grad, query_rows, preferred_element_type=jnp.float32
    )
    project_grad = jnp.stack(
        [
            gate_grad.reshape(user_count, hist_len, local_heads, HEAD),
            value_grad,
            query_grad,
            key_grad,
        ],
        3,
    ).reshape(tok_rows, 4 * local_width)
    pre_grad = (project_grad * silu_grad(pre_act)).astype(jnp.bfloat16)
    grad_in_local = lax.dot_general(
        normed, pre_grad, (((0,), (0,)), ((), ())), preferred_element_type=jnp.float32
    )
    neg_raw = logit_scale * lax.dot_general(
        logit_grads, user_rounded, (((0,), (0,)), ((), ())), preferred_element_type=jnp.float32
    )
    target_raw = jnp.where(
        owned_rows[:, None], logit_scale * positive_grad[:, None] * user_float, 0.0
    )
    target_slot = jnp.where(owned_rows, target_local, item_rows)
    pieces = lax.axis_size("dp")
    table_share = item_rows // pieces
    row_raw = segment_rows(neg_raw, neg_local, 0, item_rows) + segment_rows(
        target_raw, target_slot, 0, item_rows
    )
    totals = lax.psum((grad_in_local, grad_out_local, row_raw), "dp")
    dp_index = lax.axis_index("dp")
    in_rows = model_width // pieces
    grad_w_in = lax.dynamic_slice_in_dim(totals[0], dp_index * in_rows, in_rows, 0)
    grad_w_out = lax.dynamic_slice_in_dim(totals[1], dp_index * in_rows, in_rows, 1)
    own_first = dp_index * table_share
    grad_table = project_rows(
        lax.dynamic_slice_in_dim(totals[2], own_first, table_share, 0),
        lax.dynamic_slice_in_dim(item_unit, own_first, table_share, 0),
        lax.dynamic_slice_in_dim(item_inverse, own_first, table_share, 0),
    )
    return (token_loss, grad_w_in, grad_w_out, grad_table)


def solution(mesh):
    placed = (
        P("dp", None),
        P("dp"),
        P(None, "neg"),
        P("neg", None),
        P("dp"),
        P("neg"),
        P("neg", None),
    )
    return jax.shard_map(
        on_device,
        mesh=mesh,
        in_specs=placed,
        out_specs=(P("dp"), P("dp", "neg"), P("neg", "dp"), P(("neg", "dp"), None)),
        check_vma=False,
    )
```

profile of v0, /device:TPU:0, one launch (start us, length us, event | category | flops | bytes accessed | tf_op | source)
XLA Modules:
  0.0 389.4 jit_solution(11614462825140905152)
XLA Ops:
  7.2 0.0 reduce-scatter.3.cloned.1.call-start
  7.3 0.8 iota_compare_fusion.1
  8.1 1.4 convert_reduce_fusion
  9.5 3.1 multiply_convert_fusion.3
  12.6 0.3 copy.19
  12.9 0.2 reshape.132
  13.1 0.5 fusion.25
  13.7 0.2 and_convert_fusion
  13.9 2.3 multiply_convert_fusion.1
  16.2 1.0 copy-done.6
  17.2 0.6 fusion.24
  17.8 0.3 copy.23
  18.2 8.7 %all-reduce.3 = (f32[768]{0:T(1024)S(1)}, f32[768]{0:T(1024)S(1)}) all-reduce(f32[768]{0:T(1024)S(1)} %reduce_sum.117, f32[768]{0:T(1024)S(1)} %reduce_sum.115), channel_id=1, replica_groups=mesh['dp'=8,'neg'=4] {'neg'}, use_global_device_ids=true, to_apply=%region_5.6 | all-reduce | flops 1536 | bytes 12288 | tf_op jit(solution)/shard_map/psum | solution.py:72
  26.9 0.1 multiply_convert_fusion.8
  26.9 0.7 copy-done.13
  27.6 1.5 fusion.26
  29.2 0.0 reduce-scatter.3.cloned.1.call-update
  29.2 0.0 reduce-scatter.5.cloned.1.call-start
  29.3 1.4 convert_element_type.62
  30.7 0.7 copy-done.2
  31.3 0.5 fusion.3
  31.8 0.6 copy-done.3
  32.4 2.5 fusion.22
  34.9 5.9 %gather_fusion = f32[768,512]{1,0:T(8,128)} fusion(f32[2048,512]{1,0:T(8,128)} %get-tuple-element.23, s32[1024]{0:T(1024)S(1)} %pad_clamp_fusion), kind=kCustom, calls=%fused_computation | custom fusion | bytes 3148800 | tf_op jit(solution)/shard_map/gather | solution.py:89
  40.9 17.3 %gather_fusion.1 = bf16[4096,512]{1,0:T(8,128)(2,1)} fusion(bf16[2048,512]{1,0:T(8,128)(2,1)S(1)} %get-tuple-element.22, s32[4096]{0:T(1024)S(1)} %get-tuple-element.30), kind=kCustom, calls=%fused_computation.1 | custom fusion | bytes 8404992 | tf_op jit(solution)/shard_map/gather | solution.py:85
  58.1 0.0 reduce-scatter.3.cloned.1.call-done
  58.2 1.4 multiply_reduce_fusion.4
  59.5 0.1 multiply_convert_fusion.9
  59.7 7.5 %all_gather.6 = bf16[768,512]{1,0:T(8,128)(2,1)S(1)} all-gather(bf16[192,512]{1,0:T(8,128)(2,1)S(1)} %multiply_convert_fusion.9), channel_id=1, replica_groups=mesh['dp'=8,'neg'=4] {'neg'}, dimensions={0}, use_global_device_ids=true | all-gather | bytes 983040 | tf_op jit(solution)/shard_map/all_gather | solution.py:82
  67.1 0.4 fusion.8
  67.6 8.9 %fusion = (f32[768]{0:T(1024)S(1)}, f32[768,4096]{1,0:T(8,128)}) fusion(s32[4096]{0:T(1024)S(1)} %copy-done.23, s32[768]{0:T(1024)S(1)} %copy-done.24, bf16[768,512]{1,0:T(8,128)(2,1)S(1)} %all_gather.6, bf16[4096,512]{1,0:T(8,128)(2,1)} %gather_fusion.1), kind=kOutput, calls=%fused_computation.6 | convolution fusion | flops 3233807616 | bytes 17586176 | tf_op jit(solution)/shard_map/dot_general | solution.py:93
  76.5 7.5 %all-reduce.2 = (f32[768]{0:T(1024)S(1)}, f32[768]{0:T(1024)S(1)}) all-reduce(f32[768]{0:T(1024)S(1)} %broadcast_multiply_fusion, f32[768]{0:T(1024)S(1)} %get-tuple-element.45), channel_id=1, replica_groups=mesh['dp'=8,'neg'=4] {'neg'}, use_global_device_ids=true, to_apply=%region_10.11 | all-reduce | flops 1536 | bytes 12288 | tf_op jit(solution)/shard_map/psum | solution.py:97
  84.0 0.6 select_multiply_fusion
  84.7 7.2 %divide_convert_fusion = bf16[768,4096]{1,0:T(8,128)(2,1)S(1)} fusion(f32[768,4096]{1,0:T(8,128)} %get-tuple-element.46, f32[768]{0:T(1024)S(1)} %get-tuple-element.33, f32[768]{0:T(1024)S(1)} %convert_element_type.74, s32[4096]{0:T(1024)S(1)} %copy-done.23, s32[768]{0:T(1024)S(1)} %copy-done.24), kind=kLoop, calls=%fused_computation.4 | loop fusion | flops 18874368 | bytes 18899968 | tf_op jit(solution)/shard_map/convert_element_type | solution.py:101
  91.8 2.7 copy-done.4
  94.5 4.6 %multiply_add_fusion = f32[768,512]{1,0:T(8,128)} fusion(bf16[768,4096]{1,0:T(8,128)(2,1)S(1)} %divide_convert_fusion, bf16[4096,512]{1,0:T(8,128)(2,1)S(1)} %copy-done.8, f32[768,512]{1,0:T(8,128)S(1)} %copy-done.5, f32[768]{0:T(1024)S(1)} %get-tuple-element.31, pred[768]{0:T(1024)(128)(4,1)S(1)} %compare_and_fusion), kind=kOutput, calls=%fused_computation.26 | convolution fusion | flops 3222798336 | bytes 13635328 | tf_op jit(solution)/shard_map/dot_general | solution.py:104
  99.1 0.0 all-reduce.6.cloned.1.call-start
  99.2 9.7 %scatter_custom_fusion.1 = f32[2049,512]{1,0:T(8,128)} fusion(s32[768]{0:T(1024)S(1)} %get-tuple-element.34, f32[]{:T(128)} %constant.22.clone.1, bf16[768,512]{1,0:T(8,128)(2,1)S(1)} %all_gather.6, f32[768]{0:T(1024)S(1)} %get-tuple-element.31, pred[768]{0:T(1024)(128)(4,1)S(1)} %compare_and_fusion), kind=kCustom, calls=%fused_computation.17 | custom fusion | flops 1572864 | bytes 4988928 | tf_op jit(solution)/shard_map/scatter-add | solution.py:37
  108.9 8.6 %fusion.28 = f32[4096,512]{1,0:T(8,128)} fusion(bf16[768,4096]{1,0:T(8,128)(2,1)} %copy-done.4, bf16[768,512]{1,0:T(8,128)(2,1)S(1)} %all_gather.6), kind=kOutput, calls=%fused_computation.91 | convolution fusion | flops 3221225472 | bytes 15466496 | tf_op jit(solution)/shard_map/dot_general | solution.py:153
  117.4 27.9 %scatter_custom_fusion = f32[2049,512]{1,0:T(8,128)} fusion(s32[4096]{0:T(1024)S(1)} %get-tuple-element.29, f32[4096,512]{1,0:T(8,128)} %fusion.28, f32[]{:T(128)} %constant.29.clone.1, f32[]{:T(128)} %constant.22.clone.1), kind=kCustom, calls=%fused_computation.7 | custom fusion | flops 4194304 | bytes 12584968 | tf_op jit(solution)/shard_map/scatter-add | solution.py:37
  145.4 6.4 %slice_add_fusion = f32[2048,512]{1,0:T(8,128)} fusion(f32[2049,512]{1,0:T(8,128)} %scatter_custom_fusion.1, f32[2049,512]{1,0:T(8,128)} %scatter_custom_fusion), kind=kLoop, calls=%fused_computation.12 | loop fusion | flops 1048576 | bytes 12582912 | tf_op jit(solution)/shard_map/add | solution.py:162
  151.8 1.2 multiply_reduce_fusion.3
  153.0 1.1 multiply_convert_fusion.7
  154.2 7.6 %all_gather.7 = bf16[768,512]{1,0:T(8,128)(2,1)S(1)} all-gather(bf16[192,512]{1,0:T(8,128)(2,1)S(1)} %multiply_convert_fusion.7), channel_id=1, replica_groups=mesh['dp'=8,'neg'=4] {'neg'}, dimensions={0}, use_global_device_ids=true | all-gather | bytes 983040 | tf_op jit(solution)/shard_map/all_gather | solution.py:109
  161.8 1.2 fusion.27
  163.0 0.4 fusion.23
  163.4 7.5 %all-reduce.1 = (f32[768]{0:T(1024)S(1)}, f32[768]{0:T(1024)S(1)}) all-reduce(f32[768]{0:T(1024)S(1)} %get-tuple-element.7, f32[768]{0:T(1024)S(1)} %get-tuple-element.6), channel_id=1, replica_groups=mesh['dp'=8,'neg'=4] {'neg'}, use_global_device_ids=true, to_apply=%region_18.19 | all-reduce | flops 1536 | bytes 12288 | tf_op jit(solution)/shard_map/psum | solution.py:118
  170.9 0.1 multiply_convert_fusion.6
  171.0 0.1 reshape.134
  171.1 0.3 convolution_bitcast_fusion.2
  171.4 3.1 multiply_convert_fusion
  174.5 0.3 convolution_bitcast_fusion
  174.9 0.5 convolution_bitcast_fusion.1
  175.4 0.2 stack_reshape.3
  175.7 0.1 pad_maximum_fusion
  175.8 2.8 copy.29
  178.6 3.5 reshape.173
  182.1 3.5 fusion.14
  185.7 0.1 dynamic-slice.3
  185.7 190.7 %all-reduce.6.cloned.1.call-done = (f32[512,512]{1,0:T(8,128)}, f32[128,512]{0,1:T(8,128)}, f32[2048,512]{1,0:T(8,128)}) async-done(((f32[512,512]{1,0:T(8,128)}, f32[128,512]{0,1:T(8,128)}, f32[2048,512]{1,0:T(8,128)}), (f32[512,512]{1,0:T(8,128)}, f32[128,512]{0,1:T(8,128)}, f32[2048,512]{1,0:T(8,128)})) %all-reduce.6.cloned.1.call-update) | async-done | bytes 5505040 | tf_op jit(solution)/shard_map/psum | solution.py:165
  376.5 1.6 constant_dynamic-slice_fusion.1
  378.0 1.4 constant_dynamic-slice_fusion
  379.4 1.3 multiply_reduce_fusion.1
  380.7 2.1 subtract_multiply_fusion
  (66 shorter events, 0.4 us)
Async XLA Ops:
  7.2 2.3 copy-start
  7.2 51.0 %reduce-scatter.3.cloned.1.call-start = ((), (), s32[]{:S(2)}) async-start(), calls=%async_computation.2 | async-start | bytes 1966080 | tf_op jit(solution)/shard_map/reduce_scatter | solution.py:79
  13.6 2.5 copy-start.16
  13.6 2.5 copy-start.18
  13.6 2.5 copy-start.20
  13.7 13.2 %copy-start.9 = (f32[16,8,2,384]{3,1,2,0:T(8,128)}, f32[16,8,2,384]{3,1,2,0:T(8,128)S(1)}, u32[]{:S(2)}) copy-start(f32[16,8,2,384]{3,1,2,0:T(8,128)S(1)} %copy.35) | copy-start | bytes 1179652
  13.9 2.3 copy-start.15
  16.1 1.1 copy-start.6
  16.2 11.5 %copy-start.22 = (bf16[128,512]{1,0:T(8,128)(2,1)S(1)}, bf16[128,512]{1,0:T(8,128)(2,1)}, u32[]{:S(2)}) copy-start(bf16[128,512]{1,0:T(8,128)(2,1)} %param.10) | copy-start | bytes 393220
  18.1 11.1 %copy-start.11 = (bf16[768,512]{1,0:T(8,128)(2,1)S(1)}, bf16[768,512]{1,0:T(8,128)(2,1)}, u32[]{:S(2)}) copy-start(bf16[768,512]{1,0:T(8,128)(2,1)} %param.7) | copy-start | bytes 2359300
  26.9 0.7 copy-start.13
  29.2 1.5 copy-start.24
  29.2 2.2 copy-start.2
  29.2 122.6 %reduce-scatter.5.cloned.1.call-start = ((), (), s32[]{:S(2)}) async-start(), calls=%async_computation.3 | async-start | bytes 1966080 | tf_op jit(solution)/shard_map/reduce_scatter | solution.py:107
  30.6 1.7 copy-start.3
  34.9 5.9 %copy-start.23 = (s32[4096]{0:T(1024)S(1)}, s32[4096]{0:T(1024)}, u32[]{:S(2)}) copy-start(s32[4096]{0:T(1024)} %param.12) | copy-start | bytes 49156
  58.1 9.0 %copy-start.5 = (f32[768,512]{1,0:T(8,128)S(1)}, f32[768,512]{1,0:T(8,128)}, u32[]{:S(2)}) copy-start(f32[768,512]{1,0:T(8,128)} %gather_fusion) | copy-start | bytes 4718596
  84.7 9.9 %copy-start.8 = (bf16[4096,512]{1,0:T(8,128)(2,1)S(1)}, bf16[4096,512]{1,0:T(8,128)(2,1)}, u32[]{:S(2)}) copy-start(bf16[4096,512]{1,0:T(8,128)(2,1)} %gather_fusion.1) | copy-start | bytes 12582916
  91.8 2.7 copy-start.4
  99.1 277.3 %all-reduce.6.cloned.1.call-start = ((), (), s32[]{:S(2)}) async-start(), calls=%async_computation.4 | async-start | bytes 11010048 | tf_op jit(solution)/shard_map/psum | solution.py:165
  151.8 10.0 %copy-start.14 = (bf16[768,128]{0,1:T(8,128)(2,1)S(1)}, bf16[768,128]{0,1:T(8,128)(2,1)}, u32[]{:S(2)}) copy-start(bf16[768,128]{0,1:T(8,128)(2,1)} %copy-done.13) | copy-start | bytes 589828
  151.8 11.2 %copy-start.10 = (f32[16,8,2,384]{3,1,2,0:T(8,128)S(1)}, f32[16,8,2,384]{3,1,2,0:T(8,128)}, u32[]{:S(2)}) copy-start(f32[16,8,2,384]{3,1,2,0:T(8,128)} %copy-done.9) | copy-start | bytes 1179652
  161.8 9.3 %copy-start.7 = (bf16[2,2,384,384]{3,2,1,0:T(8,128)(2,1)S(1)}, bf16[2,2,384,384]{3,2,1,0:T(8,128)(2,1)}, u32[]{:S(2)}) copy-start(bf16[2,2,384,384]{3,2,1,0:T(8,128)(2,1)} %copy-done.6) | copy-start | bytes 3538948
  163.0 8.4 %copy-start.21 = (bf16[2,384,2,1,64]{1,0,4,3,2:T(2,128)(2,1)S(1)}, bf16[2,384,2,1,64]{1,0,4,3,2:T(2,128)(2,1)}, u32[]{:S(2)}) copy-start(bf16[2,384,2,1,64]{1,0,4,3,2:T(2,128)(2,1)} %copy-done.20) | copy-start | bytes 589828
  171.4 3.2 copy-start.19
  171.4 3.5 copy-start.17
  178.6 3.5 copy-start.12
  185.6 197.2 %copy-start.1 = (bf16[512,512]{1,0:T(8,128)(2,1)S(1)}, bf16[512,512]{1,0:T(8,128)(2,1)}, u32[]{:S(2)}) copy-start(bf16[512,512]{1,0:T(8,128)(2,1)} %param.9) | copy-start | bytes 1572868
Sparse Core Ops, SparseCore 0:
  29.3 28.2 reduce-scatter.2
  99.3 28.2 reduce-scatter.4
  185.8 190.6 all-reduce.5
where the time goes:
time: 390 us; the launch traced here: 389 us
  waiting for transfers between devices  191 us (49%)
  other arithmetic  67.2 us (17%)
  local copies, waits for them, and re-layouts  39.4 us (10%)
  matrix products  38.8 us (10%)
  blocking collectives  38.8 us (10%)
  between operations  14.2 us (4%)
    psum x1, waiting for transfers between devices, on_device(): totals = lax.psum((grad_in_local, grad_out_local, row_raw), 'dp')  191 us
    scatter-add x2, other arithmetic, segment_rows(): return jax.ops.segment_sum(values, placed, row_count + 1)[:row_count]  37.6 us
    gather x1, local copies, waits for them, and re-layouts, on_device(): neg_rounded = item_unit.astype(jnp.bfloat16)[neg_local]  17.3 us
    dot_general x1, matrix products, on_device(): lax.dot_general(user_rounded, neg_rounded, (((1,), (1,)), ((), ())), pref...  8.91 us
    psum x1, blocking collectives, on_device(): lax.psum((jnp.sum(attended, -1), jnp.sum(attended * attended, -1)), 'neg')  8.69 us
    dot_general x1, matrix products, on_device(): lax.dot_general(logit_grads, user_rounded, (((0,), (0,)), ((), ())), pref...  8.57 us
  transfers between devices with their start and end apart: 3, of which 1 were waited for; matrix products, arithmetic and copies ran while one was open for 21% of the time, Pallas kernels for 0%

commit v1 on v0

--- a/solution.py
+++ b/solution.py
@@ -31,10 +31,14 @@
     return (raw_rows - unit_part * jnp.sum(raw_rows * unit_part, -1, keepdims=True)) * inverse
 
 
-def segment_rows(values, slots, first_row, row_count):
-    inside = (slots >= first_row) & (slots < first_row + row_count)
-    placed = jnp.where(inside, slots - first_row, row_count)
-    return jax.ops.segment_sum(values, placed, row_count + 1)[:row_count]
+def count_rows(slots, row_count):
+    lanes = 128
+    coarse = (slots // lanes)[None, :] == jnp.arange(row_count // lanes, dtype=jnp.int32)[:, None]
+    fine = (slots % lanes)[:, None] == jnp.arange(lanes, dtype=jnp.int32)[None, :]
+    table = jnp.dot(
+        coarse.astype(jnp.bfloat16), fine.astype(jnp.bfloat16), preferred_element_type=jnp.float32
+    )
+    return table.reshape(1, row_count)
 
 
 def on_device(history, lengths, w_in, w_out, target_ids, negative_ids, item_table):
@@ -76,39 +80,47 @@
     gate_flat = gate_rows.reshape(tok_rows, local_width).astype(jnp.float32)
     mixed_rows = (centred * gate_flat).astype(jnp.bfloat16)
     branch = jnp.dot(mixed_rows, w_out, preferred_element_type=jnp.float32)
-    branch_part = lax.psum_scatter(branch, "neg", scatter_dimension=0, tiled=True)
+    branch_part = lax.psum_scatter(
+        branch.astype(jnp.bfloat16), "neg", scatter_dimension=0, tiled=True
+    ).astype(jnp.float32)
     inputs_part = lax.dynamic_slice_in_dim(inputs_float, share_start, share_rows, 0)
     user_unit, user_inverse = normalize_rows(inputs_part + branch_part)
     user_rounded = lax.all_gather(user_unit.astype(jnp.bfloat16), "neg", axis=0, tiled=True)
     item_unit, item_inverse = normalize_rows(item_table.astype(jnp.float32))
-    neg_local = negative_ids - item_base
-    neg_rounded = item_unit.astype(jnp.bfloat16)[neg_local]
-    target_local = target_ids - item_base
-    owned_rows = (target_local >= 0) & (target_local < item_rows)
-    target_unit = jnp.where(
-        owned_rows[:, None], item_unit[jnp.clip(target_local, 0, item_rows - 1)], 0.0
-    )
-    user_float = user_rounded.astype(jnp.float32)
-    positive_part = logit_scale * jnp.sum(user_float * target_unit, -1)
+    item_rounded = item_unit.astype(jnp.bfloat16)
+    row_counts = count_rows(negative_ids - item_base, item_rows)
+    is_target = (target_ids - item_base)[:, None] == jnp.arange(item_rows, dtype=jnp.int32)[None, :]
     logits = logit_scale * lax.dot_general(
-        user_rounded, neg_rounded, (((1,), (1,)), ((), ())), preferred_element_type=jnp.float32
-    )
-    exp_terms = jnp.where(target_ids[:, None] != negative_ids[None, :], jnp.exp(logits), 0.0)
-    positive, negative_sum = lax.psum((positive_part, jnp.sum(exp_terms, -1)), "neg")
+        user_rounded, item_rounded, (((1,), (1,)), ((), ())), preferred_element_type=jnp.float32
+    )
+    exp_terms = jnp.where(is_target, 0.0, row_counts * jnp.exp(logits))
+    positive, negative_sum = lax.psum(
+        (jnp.sum(jnp.where(is_target, logits, 0.0), -1), jnp.sum(exp_terms, -1)), "neg"
+    )
     partition_sum = jnp.exp(positive) + negative_sum
     live_rows = live_slots.reshape(tok_rows).astype(jnp.float32)
     token_loss = live_rows * (jnp.log(partition_sum) - positive)
-    logit_grads = (live_rows[:, None] * exp_terms / partition_sum[:, None]).astype(jnp.bfloat16)
     positive_grad = live_rows * (jnp.exp(positive) / partition_sum - 1.0)
-    unit_part = (
-        logit_scale * jnp.dot(logit_grads, neg_rounded, preferred_element_type=jnp.float32)
-        + logit_scale * positive_grad[:, None] * target_unit
-    )
-    unit_grad = lax.psum_scatter(unit_part, "neg", scatter_dimension=0, tiled=True)
+    row_factor = live_rows / partition_sum
+    coefficients = jnp.where(
+        is_target, positive_grad[:, None], row_factor[:, None] * exp_terms
+    ).astype(jnp.bfloat16)
+    unit_part = logit_scale * jnp.dot(
+        coefficients, item_rounded, preferred_element_type=jnp.float32
+    )
+    row_raw = logit_scale * lax.dot_general(
+        coefficients, user_rounded, (((0,), (0,)), ((), ())), preferred_element_type=jnp.float32
+    )
+    row_total = lax.psum_scatter(
+        row_raw.astype(jnp.bfloat16), "dp", scatter_dimension=0, tiled=True
+    ).astype(jnp.float32)
+    unit_grad = lax.psum_scatter(
+        unit_part.astype(jnp.bfloat16), "neg", scatter_dimension=0, tiled=True
+    ).astype(jnp.float32)
     output_part = project_rows(unit_grad, user_unit, user_inverse).astype(jnp.bfloat16)
     output_rounded = lax.all_gather(output_part, "neg", axis=0, tiled=True)
     grad_out_local = lax.dot_general(
-        mixed_rows, output_rounded, (((0,), (0,)), ((), ())), preferred_element_type=jnp.float32
+        output_rounded, mixed_rows, (((0,), (0,)), ((), ())), preferred_element_type=jnp.float32
     )
     mixed_grad = lax.dot_general(
         output_rounded, w_out, (((1,), (1,)), ((), ())), preferred_element_type=jnp.float32
@@ -150,26 +162,20 @@
     grad_in_local = lax.dot_general(
         normed, pre_grad, (((0,), (0,)), ((), ())), preferred_element_type=jnp.float32
     )
-    neg_raw = logit_scale * lax.dot_general(
-        logit_grads, user_rounded, (((0,), (0,)), ((), ())), preferred_element_type=jnp.float32
-    )
-    target_raw = jnp.where(
-        owned_rows[:, None], logit_scale * positive_grad[:, None] * user_float, 0.0
-    )
-    target_slot = jnp.where(owned_rows, target_local, item_rows)
-    pieces = lax.axis_size("dp")
-    table_share = item_rows // pieces
-    row_raw = segment_rows(neg_raw, neg_local, 0, item_rows) + segment_rows(
-        target_raw, target_slot, 0, item_rows
-    )
-    totals = lax.psum((grad_in_local, grad_out_local, row_raw), "dp")
-    dp_index = lax.axis_index("dp")
-    in_rows = model_width // pieces
-    grad_w_in = lax.dynamic_slice_in_dim(totals[0], dp_index * in_rows, in_rows, 0)
-    grad_w_out = lax.dynamic_slice_in_dim(totals[1], dp_index * in_rows, in_rows, 1)
-    own_first = dp_index * table_share
+    grad_w_in = lax.psum_scatter(
+        grad_in_local.astype(jnp.bfloat16), "dp", scatter_dimension=0, tiled=True
+    ).astype(jnp.float32)
+    grad_w_out = (
+        lax.psum_scatter(
+            grad_out_local.astype(jnp.bfloat16), "dp", scatter_dimension=0, tiled=True
+        )
+        .astype(jnp.float32)
+        .T
+    )
+    table_share = item_rows // lax.axis_size("dp")
+    own_first = lax.axis_index("dp") * table_share
     grad_table = project_rows(
-        lax.dynamic_slice_in_dim(totals[2], own_first, table_share, 0),
+        row_total,
         lax.dynamic_slice_in_dim(item_unit, own_first, table_share, 0),
         lax.dynamic_slice_in_dim(item_inverse, own_first, table_share, 0),
     )

time: 390 us -> 361 us (0.926)
  other arithmetic: 67.2 us -> 28.4 us
  waiting for transfers between devices: 191 us -> 228 us
  local copies, waits for them, and re-layouts: 39.4 us -> 15.5 us
    reduce_scatter x2 -> x5, waiting for transfers between devices: 0.02 us -> 228 us  [the longest x1 69.3 us: on_device(): lax.psum_scatter(row_raw.astype(jnp.bfloat16), 'dp', scatter_dimension=0,...]
    psum x1 -> x0, waiting for transfers between devices: 191 us -> none  [on_device(): totals = lax.psum((grad_in_local, grad_out_local, row_raw), 'dp')]
    scatter-add x2 -> x0, other arithmetic: 37.6 us -> none  [segment_rows(): return jax.ops.segment_sum(values, placed, row_count + 1)[:row_count]]
    gather x2 -> x0, local copies, waits for them, and re-layouts: 23.2 us -> none  [the longest x1 17.3 us: on_device(): neg_rounded = item_unit.astype(jnp.bfloat16)[neg_local]]
    dot_general x4 -> x5, matrix products: 23.2 us -> 15 us  [the longest x1 5.25 us: on_device(): lax.dot_general(coefficients, user_rounded, (((0,), (0,)), ((), ())), pre...]
    add x1 -> x0, other arithmetic: 6.41 us -> none  [on_device(): segment_rows(neg_raw, neg_local, 0, item_rows)]
    convert_element_type x3 -> x2, other arithmetic: 9.71 us -> 5.79 us  [the longest x1 4.28 us: on_device(): coefficients = jnp.where(is_target, positive_grad[:, None], row_factor[:,...]
  transfers between devices with their start and end apart: 3 -> 5, of which waited for: 1 -> 5; matrix products, arithmetic and copies ran while one was open for 21% -> 5% of each run, Pallas kernels for 0% -> 0%
where the time goes in v1:
time: 361 us; the launch traced here: 360 us
  waiting for transfers between devices  228 us (63%)
  blocking collectives  38.5 us (11%)
  matrix products  35.7 us (10%)
  other arithmetic  28.4 us (8%)
  local copies, waits for them, and re-layouts  15.5 us (4%)
  between operations  14.2 us (4%)
    reduce_scatter x1, waiting for transfers between devices, on_device(): lax.psum_scatter(row_raw.astype(jnp.bfloat16), 'dp', scatter_dimension=0,...  69.3 us
    reduce_scatter x1, waiting for transfers between devices, on_device(): lax.psum_scatter(grad_in_local.astype(jnp.bfloat16), 'dp', scatter_dimens...  64.1 us
    reduce_scatter x1, waiting for transfers between devices, on_device(): lax.psum_scatter(grad_out_local.astype(jnp.bfloat16), 'dp', scatter_dimen...  50.9 us
    reduce_scatter x1, waiting for transfers between devices, on_device(): lax.psum_scatter(unit_part.astype(jnp.bfloat16), 'neg', scatter_dimension...  23.7 us
    reduce_scatter x1, waiting for transfers between devices, on_device(): lax.psum_scatter(branch.astype(jnp.bfloat16), 'neg', scatter_dimension=0,...  19.7 us
    psum x1, blocking collectives, on_device(): lax.psum((jnp.sum(attended, -1), jnp.sum(attended * attended, -1)), 'neg')  8.57 us
    reshape x2, local copies, waits for them, and re-layouts, on_device(): project_grad = jnp.stack([gate_grad.reshape(user_count, hist_len, local_h...  8.55 us
    all_gather x1, blocking collectives, on_device(): output_rounded = lax.all_gather(output_part, 'neg', axis=0, tiled=True)  8.19 us
  transfers between devices with their start and end apart: 5, of which 5 were waited for; matrix products, arithmetic and copies ran while one was open for 5% of the time, Pallas kernels for 0%

profile of v1, /device:TPU:0, one launch (start us, length us, event | category | flops | bytes accessed | tf_op | source)
XLA Modules:
  0.0 360.2 jit_solution(10533729795031104178)
XLA Ops:
  7.2 0.0 reduce-scatter.6.cloned.1.call-start
  7.3 0.8 iota_compare_fusion.8
  8.1 1.4 convert_reduce_fusion
  9.5 3.1 multiply_convert_fusion.5
  12.6 0.3 copy.19
  12.9 0.2 reshape.123
  13.1 0.5 fusion.24
  13.7 0.2 and_convert_fusion
  13.9 2.2 multiply_convert_fusion.2
  16.2 0.6 fusion.23
  16.8 0.3 copy.23
  17.1 0.1 copy-done.3
  17.3 8.6 %all-reduce.2 = (f32[768]{0:T(1024)S(1)}, f32[768]{0:T(1024)S(1)}) all-reduce(f32[768]{0:T(1024)S(1)} %reduce_sum.117, f32[768]{0:T(1024)S(1)} %reduce_sum.115), channel_id=1, replica_groups=mesh['dp'=8,'neg'=4] {'neg'}, use_global_device_ids=true, to_apply=%region_5.6 | all-reduce | flops 1536 | bytes 12288 | tf_op jit(solution)/shard_map/psum | solution.py:76
  25.9 0.1 multiply_convert_fusion.9
  26.0 0.7 copy-done.10
  26.6 1.3 convolution_convert_fusion
  27.9 0.0 reduce-scatter.6.cloned.1.call-update
  27.9 0.0 reduce-scatter.8.cloned.1.call-start
  28.0 0.6 lt.37
  28.5 1.4 convert_element_type.85
  29.9 0.7 add_select_fusion.1
  30.7 0.7 fusion.3
  31.4 0.5 fusion.1
  31.9 19.7 %reduce-scatter.6.cloned.1.call-done = bf16[192,512]{1,0:T(8,128)(2,1)} async-done(((bf16[768,512]{1,0:T(8,128)(2,1)}), bf16[192,512]{1,0:T(8,128)(2,1)}) %reduce-scatter.6.cloned.1.call-update) | async-done | bytes 196624 | tf_op jit(solution)/shard_map/reduce_scatter | solution.py:83
  51.6 1.2 multiply_reduce_fusion.2
  52.8 1.2 multiply_convert_fusion.10
  54.0 8.0 %all_gather.6 = bf16[768,512]{1,0:T(8,128)(2,1)S(1)} all-gather(bf16[192,512]{1,0:T(8,128)(2,1)S(1)} %multiply_convert_fusion.10), channel_id=1, replica_groups=mesh['dp'=8,'neg'=4] {'neg'}, dimensions={0}, use_global_device_ids=true | all-gather | bytes 983040 | tf_op jit(solution)/shard_map/all_gather | solution.py:88
  62.0 5.2 %fusion = (f32[768]{0:T(1024)S(1)}, f32[768]{0:T(1024)S(1)}, f32[768,2048]{1,0:T(8,128)}) fusion(f32[2048]{0:T(1024)S(1)} %fusion.3, s32[768]{0:T(1024)S(1)} %broadcast_subtract_fusion, bf16[768,512]{1,0:T(8,128)(2,1)S(1)} %all_gather.6, f32[2048]{0:T(1024)S(1)} %add_rsqrt_fusion, bf16[2048,512]{1,0:T(8,128)(2,1)S(1)} %copy-done.1), kind=kOutput, calls=%fused_computation.6 | convolution fusion | flops 1624766976 | bytes 9200640 | tf_op jit(solution)/shard_map/dot_general | solution.py:93
  67.2 6.8 %all-reduce.1 = (f32[768]{0:T(1024)S(1)}, f32[768]{0:T(1024)S(1)}) all-reduce(f32[768]{0:T(1024)S(1)} %get-tuple-element.5, f32[768]{0:T(1024)S(1)} %get-tuple-element.4), channel_id=1, replica_groups=mesh['dp'=8,'neg'=4] {'neg'}, use_global_device_ids=true, to_apply=%region_10.11 | all-reduce | flops 1536 | bytes 12288 | tf_op jit(solution)/shard_map/psum | solution.py:97
  74.1 0.6 convert_divide_fusion
  74.7 4.3 %select_convert_fusion = bf16[768,2048]{1,0:T(8,128)(2,1)S(1)} fusion(f32[768,2048]{1,0:T(8,128)} %get-tuple-element.37, f32[768]{0:T(1024)S(1)} %get-tuple-element.26, bf16[768]{0:T(1024)(128)(2,1)S(1)} %add_select_fusion.2, f32[2048]{0:T(1024)S(1)} %fusion.3, s32[768]{0:T(1024)S(1)} %broadcast_subtract_fusion), kind=kLoop, calls=%fused_computation | loop fusion | flops 9437184 | bytes 9453056 | tf_op jit(solution)/shard_map/convert_element_type | solution.py:107
  79.0 1.7 copy-done.9
  80.7 2.8 multiply_convert_fusion.4
  83.5 0.0 reduce-scatter.12.cloned.1.call-start
  83.5 23.7 %reduce-scatter.8.cloned.1.call-done = bf16[192,512]{1,0:T(8,128)(2,1)} async-done(((bf16[768,512]{1,0:T(8,128)(2,1)}), bf16[192,512]{1,0:T(8,128)(2,1)}) %reduce-scatter.8.cloned.1.call-update) | async-done | bytes 196624 | tf_op jit(solution)/shard_map/reduce_scatter | solution.py:117
  107.2 1.3 fusion.10
  108.5 1.3 fusion.12
  109.8 8.2 %all_gather.7 = bf16[768,512]{1,0:T(8,128)(2,1)S(1)} all-gather(bf16[192,512]{1,0:T(8,128)(2,1)S(1)} %fusion.12), channel_id=1, replica_groups=mesh['dp'=8,'neg'=4] {'neg'}, dimensions={0}, use_global_device_ids=true | all-gather | bytes 983040 | tf_op jit(solution)/shard_map/all_gather | solution.py:121
  118.0 3.0 fusion.22
  121.0 6.9 %all-reduce = (f32[768]{0:T(1024)S(1)}, f32[768]{0:T(1024)S(1)}) all-reduce(f32[768]{0:T(1024)} %get-tuple-element.9, f32[768]{0:T(1024)} %get-tuple-element.8), channel_id=1, replica_groups=mesh['dp'=8,'neg'=4] {'neg'}, use_global_device_ids=true, to_apply=%region_18.19 | all-reduce | flops 1536 | bytes 12288 | tf_op jit(solution)/shard_map/psum | solution.py:130
  128.0 1.9 multiply_convert_fusion.8
  129.9 1.7 reshape.125
  131.5 3.3 multiply_convert_fusion.1
  134.9 1.1 convolution_bitcast_fusion
  136.0 1.3 convolution_bitcast_fusion.1
  137.2 1.1 convolution_bitcast_fusion.2
  138.4 1.1 convolution_convert_fusion.2
  139.4 1.2 stack_reshape.3
  140.7 2.5 pad_maximum_fusion
  143.2 4.1 %copy.29 = f32[2,384,2,4,64]{4,3,2,1,0:T(4,128)} copy(f32[2,384,2,4,64]{1,4,2,0,3:T(8,128)} %pad_maximum_fusion) | data formatting | bytes 3145728 | tf_op jit(solution)/shard_map/reshape | solution.py:160
  147.3 4.4 %reshape.128 = f32[768,512]{1,0:T(8,128)} reshape(f32[2,384,2,4,64]{4,3,2,1,0:T(4,128)} %copy.29) | data formatting | bytes 3145728 | tf_op jit(solution)/shard_map/reshape | solution.py:160
  151.8 0.0 reduce-scatter.10.cloned.1.call-start
  151.9 3.8 %convolution_convert_fusion.1 = bf16[512,512]{1,0:T(8,128)(2,1)} fusion(f32[768,512]{1,0:T(8,128)} %reshape.128, f32[768,512]{1,0:T(8,128)} %get-tuple-element.33, bf16[768,512]{1,0:T(8,128)(2,1)S(1)} %copy-done.7, f32[768]{0:T(1024)S(1)} %copy-done.26, f32[768]{0:T(1024)S(1)} %copy-done.24), kind=kOutput, calls=%fused_computation.22 | convolution fusion | flops 408027136 | bytes 4462592 | tf_op jit(solution)/shard_map/dot_general | solution.py:162
  155.7 0.0 reduce-scatter.14.cloned.1.call-start
  155.7 5.2 %multiply_convert_fusion = bf16[2048,512]{1,0:T(8,128)(2,1)} fusion(bf16[768,2048]{1,0:T(8,128)(2,1)} %copy-done.9, bf16[768,512]{1,0:T(8,128)(2,1)} %copy-done.18), kind=kOutput, calls=%fused_computation.8 | convolution fusion | flops 1612709888 | bytes 6029312 | tf_op jit(solution)/shard_map/dot_general | solution.py:111
  161.0 0.1 dynamic-slice.3
  161.1 2.3 convert_multiply_fusion
  163.3 50.9 %reduce-scatter.12.cloned.1.call-done = bf16[64,128]{1,0:T(8,128)(2,1)} async-done(((bf16[512,128]{1,0:T(8,128)(2,1)}), bf16[64,128]{1,0:T(8,128)(2,1)}) %reduce-scatter.12.cloned.1.call-update) | async-done | bytes 16400 | tf_op jit(solution)/shard_map/reduce_scatter | solution.py:169
  214.2 1.3 convert_bitcast_fusion
  215.5 64.1 %reduce-scatter.10.cloned.1.call-done = bf16[64,512]{1,0:T(8,128)(2,1)} async-done(((bf16[512,512]{1,0:T(8,128)(2,1)}), bf16[64,512]{1,0:T(8,128)(2,1)}) %reduce-scatter.10.cloned.1.call-update) | async-done | bytes 65552 | tf_op jit(solution)/shard_map/reduce_scatter | solution.py:165
  279.6 1.5 convert_element_type.107
  281.1 69.3 %reduce-scatter.14.cloned.1.call-done = bf16[256,512]{1,0:T(8,128)(2,1)} async-done(((bf16[2048,512]{1,0:T(8,128)(2,1)}), bf16[256,512]{1,0:T(8,128)(2,1)}) %reduce-scatter.14.cloned.1.call-update) | async-done | bytes 262160 | tf_op jit(solution)/shard_map/reduce_scatter | solution.py:114
  350.4 1.3 fusion.8
  351.6 2.1 fusion.9
  (68 shorter events, 0.4 us)
Async XLA Ops:
  7.2 2.4 copy-start
  7.2 44.4 %reduce-scatter.6.cloned.1.call-start = ((), (), s32[]{:S(2)}) async-start(), calls=%async_computation.5 | async-start | bytes 983040 | tf_op jit(solution)/shard_map/reduce_scatter | solution.py:83
  9.5 3.1 copy-start.23
  9.5 3.1 copy-start.25
  13.6 2.5 copy-start.13
  13.7 2.5 copy-start.15
  13.7 2.5 copy-start.19
  13.7 12.2 %copy-start.5 = (f32[16,8,2,384]{3,1,2,0:T(8,128)}, f32[16,8,2,384]{3,1,2,0:T(8,128)S(1)}, u32[]{:S(2)}) copy-start(f32[16,8,2,384]{3,1,2,0:T(8,128)S(1)} %copy.35) | copy-start | bytes 1179652
  13.9 2.3 copy-start.12
  16.2 1.1 copy-start.3
  16.2 10.4 %copy-start.20 = (bf16[128,512]{1,0:T(8,128)(2,1)S(1)}, bf16[128,512]{1,0:T(8,128)(2,1)}, u32[]{:S(2)}) copy-start(bf16[128,512]{1,0:T(8,128)(2,1)} %param.10) | copy-start | bytes 393220
  16.7 11.8 %copy-start.6 = (bf16[768,512]{1,0:T(8,128)(2,1)S(1)}, bf16[768,512]{1,0:T(8,128)(2,1)}, u32[]{:S(2)}) copy-start(bf16[768,512]{1,0:T(8,128)(2,1)} %param.7) | copy-start | bytes 2359300
  17.2 8.7 %copy-start.2 = (f32[16,8,2,384]{3,1,2,0:T(8,128)}, f32[16,8,2,384]{3,1,2,0:T(8,128)S(1)}, u32[]{:S(2)}) copy-start(f32[16,8,2,384]{3,1,2,0:T(8,128)S(1)} %copy.34) | copy-start | bytes 1179652
  25.9 0.7 copy-start.10
  27.9 3.5 copy-start.22
  27.9 3.5 copy-start.1
  27.9 79.3 %reduce-scatter.8.cloned.1.call-start = ((), (), s32[]{:S(2)}) async-start(), calls=%async_computation.6 | async-start | bytes 983040 | tf_op jit(solution)/shard_map/reduce_scatter | solution.py:117
  62.0 5.2 %copy-start.18 = (bf16[768,512]{1,0:T(8,128)(2,1)}, bf16[768,512]{1,0:T(8,128)(2,1)S(1)}, u32[]{:S(2)}) copy-start(bf16[768,512]{1,0:T(8,128)(2,1)S(1)} %all_gather.6) | copy-start | bytes 2359300
  62.0 12.0 %copy-start.21 = (pred[768]{0:T(1024)(128)(4,1)S(1)}, pred[768]{0:T(1024)(128)(4,1)}, u32[]{:S(2)}) copy-start(pred[768]{0:T(1024)(128)(4,1)} %lt.37) | copy-start | bytes 2308
  79.0 1.7 copy-start.9
  80.7 26.6 %copy-start.8 = (bf16[192,512]{1,0:T(8,128)(2,1)S(1)}, bf16[192,512]{1,0:T(8,128)(2,1)}, u32[]{:S(2)}) copy-start(bf16[192,512]{1,0:T(8,128)(2,1)} %reduce-scatter.6.cloned.1.call-done) | copy-start | bytes 589828
  83.5 130.7 %reduce-scatter.12.cloned.1.call-start = ((), (), s32[]{:S(2)}) async-start(), calls=%async_computation.8 | async-start | bytes 147456 | tf_op jit(solution)/shard_map/reduce_scatter | solution.py:169
  131.5 3.3 copy-start.16
  131.5 4.4 %copy-start.14 = (bf16[2,384,2,1,64]{1,0,4,3,2:T(2,128)(2,1)S(1)}, bf16[2,384,2,1,64]{1,0,4,3,2:T(2,128)(2,1)}, u32[]{:S(2)}) copy-start(bf16[2,384,2,1,64]{1,0,4,3,2:T(2,128)(2,1)} %copy-done.13) | copy-start | bytes 589828
  134.9 2.4 copy-start.4
  134.9 2.4 copy-start.17
  136.0 2.4 copy-start.11
  147.3 4.5 %copy-start.7 = (bf16[768,512]{1,0:T(8,128)(2,1)S(1)}, bf16[768,512]{1,0:T(8,128)(2,1)}, u32[]{:S(2)}) copy-start(bf16[768,512]{1,0:T(8,128)(2,1)} %param.7) | copy-start | bytes 2359300
  147.3 4.5 %copy-start.24 = (f32[768]{0:T(1024)S(1)}, f32[768]{0:T(1024)}, u32[]{:S(2)}) copy-start(f32[768]{0:T(1024)} %copy-done.23) | copy-start | bytes 9220
  147.3 4.5 %copy-start.26 = (f32[768]{0:T(1024)S(1)}, f32[768]{0:T(1024)}, u32[]{:S(2)}) copy-start(f32[768]{0:T(1024)} %copy-done.25) | copy-start | bytes 9220
  151.8 127.8 %reduce-scatter.10.cloned.1.call-start = ((), (), s32[]{:S(2)}) async-start(), calls=%async_computation.7 | async-start | bytes 589824 | tf_op jit(solution)/shard_map/reduce_scatter | solution.py:165
  155.7 194.7 %reduce-scatter.14.cloned.1.call-start = ((), (), s32[]{:S(2)}) async-start(), calls=%async_computation.9 | async-start | bytes 2359296 | tf_op jit(solution)/shard_map/reduce_scatter | solution.py:114
Sparse Core Ops, SparseCore 0:
  28.0 23.4 reduce-scatter.5
  83.6 23.5 reduce-scatter.7
  151.9 62.2 reduce-scatter.11
  218.0 61.6 reduce-scatter.9
  283.0 67.3 reduce-scatter.13
